TPU v7x, 512 devices: a whole 4x8x8 slice. The times are simulated.
512 devices in a mesh: member: 16 (over x, y_lo), lat: 32 (over z, y_hi, core).
Axes of the slice: x: 4, y: 8 (y_hi: 2, y_lo: 4; y = y_hi * 4 + y_lo), z: 8, core: 2. Of those that a mesh axis runs over, the one named last changes fastest.
Arguments:
- states: bfloat16 [16, 64, 256, 256], P('member', 'lat'), may hold values from -6 to 6
- member_id: int32 [16], P('member'), may hold values from 0 to 15, each once
- member_gain: float32 [16, 256], replicated, may hold values from 0.5 to 2
- first_conv: bfloat16 [2304, 256], P('member'), may hold values from -0.125 to 0.125
- second_conv: bfloat16 [2304, 256], P('member'), may hold values from -0.125 to 0.125
- head: bfloat16 [256, 8], replicated, may hold values from -0.375 to 0.375
- target: float32 [8, 64, 256], P(None, 'lat'), may hold values from -6 to 6
- lat_start: int32 [1], replicated, may hold values from 0 to 1737
Outputs:
- score: float32 [8, 64, 256], P(None, 'lat')
- mean_score: float32 [], replicated
All inputs are finite; a program needn't handle non-finite values.
Results may differ from a plain program's by a relative error of at most 0.0018.
Values may be sent and summed in bfloat16 or wider, within the bound.
No kernel may reach another device: no remote copies, remote signals or barrier semaphores. Data moves between devices by JAX's collectives and lax.ppermute only.
A program may use at most 64 MiB of HBM per device.

v0:
```python
import jax
import jax.numpy as jnp
from jax import lax
from jax.sharding import PartitionSpec as P


def with_halo(block, sides, width):
    for axis, dim in sides:
        count = lax.axis_size(axis)
        forward = [(i, i + 1) for i in range(count - 1)]
        backward = [(target, source) for source, target in forward]
        low = lax.ppermute(
            lax.slice_in_dim(block, block.shape[dim] - width, None, axis=dim), axis, forward
        )
        high = lax.ppermute(lax.slice_in_dim(block, 0, width, axis=dim), axis, backward)
        block = jnp.concatenate([low, block, high], axis=dim)
    return block


def product(left, right):
    return jnp.dot(
        left.astype(jnp.float32),
        right.astype(jnp.float32),
        precision=lax.Precision.HIGHEST,
        preferred_element_type=jnp.float32,
    )


def patch_rows(field):
    rows, cols, chans = (field.shape[0] - 2, field.shape[1], field.shape[2])
    padded = jnp.pad(field, ((0, 0), (1, 1), (0, 0)))
    taps = [padded[dy : dy + rows, dx : dx + cols, :] for dy in range(3) for dx in range(3)]
    return jnp.concatenate(taps, axis=-1).reshape(rows * cols, 9 * chans)


def folded_conv(patches, weight_rows):
    return product(patches, lax.all_gather(weight_rows, "member", axis=0, tiled=True))


def body(states, member_id, member_gain, first_conv, second_conv, head, target, lat_start):
    rows, cols, chans = (states.shape[1], states.shape[2], states.shape[3])
    members = lax.axis_size("member")
    band = lax.axis_index("lat")
    select = (jnp.arange(members, dtype=jnp.int32)[None, :] == member_id[:, None]).astype(
        jnp.float32
    )
    gain = jnp.dot(select, member_gain, precision=lax.Precision.HIGHEST)
    start = (states[0].astype(jnp.float32) * gain[0]).astype(jnp.bfloat16)

    def with_rims(field):
        return with_halo(field, (("lat", 0),), 1)

    first_out = folded_conv(patch_rows(with_rims(start)), first_conv)
    inner = jax.nn.gelu(first_out, approximate=True).astype(jnp.bfloat16).reshape(rows, cols, -1)
    second_out = folded_conv(patch_rows(with_rims(inner)), second_conv)
    block = (start.reshape(rows * cols, chans).astype(jnp.float32) + second_out).astype(
        jnp.bfloat16
    )
    pred = product(block, head)
    pred = pred.T.reshape(-1, rows, cols).astype(jnp.bfloat16)
    eps = 0.05 / members
    factor = (1.0 - eps) / (2.0 * members * (members - 1))
    fields = lax.all_gather(pred[None], "member", axis=0, tiled=True).astype(jnp.float32)
    skill = jnp.sum(jnp.abs(fields - target[None]), axis=0) / members

    def pair_step(index, total):
        chosen = lax.dynamic_index_in_dim(fields, index, 0, keepdims=True)
        return total + jnp.sum(jnp.abs(chosen - fields), axis=0)

    spread = lax.fori_loop(0, members, pair_step, jnp.zeros_like(skill))
    score = skill - factor * spread
    row_ids = lat_start[0] + band * rows + jnp.arange(rows, dtype=jnp.int32)
    area = jnp.cos(jnp.pi * (90.0 - 0.1 * row_ids.astype(jnp.float32)) / 180.0)
    weighted, area_total = lax.psum((jnp.sum(score * area[None, :, None]), jnp.sum(area)), "lat")
    mean_score = weighted / (score.shape[0] * cols * area_total)
    return (score, mean_score)


def solution(mesh):
    placed = (
        P("member", "lat", None, None),
        P("member"),
        P(),
        P("member", None),
        P("member", None),
        P(),
        P(None, "lat", None),
        P(),
    )
    return jax.shard_map(
        body, mesh=mesh, in_specs=placed, out_specs=(P(None, "lat", None), P()), check_vma=False
    )
```

profile of v0, /device:TPU:1, one launch (start us, length us, event | category | flops | bytes accessed | tf_op | source)
XLA Modules:
  0.0 331.9 jit_solution(7354187665463545966)
XLA Ops:
  7.2 0.7 all-gather.3.cloned.1.call-update
  8.6 0.1 fusion.20
  8.7 1.0 fusion.15
  9.8 8.8 %collective-permute-start = (bf16[1,256,256]{2,1,0:T(8,128)(2,1)S(1)}, bf16[1,256,256]{2,1,0:T(8,128)(2,1)S(1)}, u32[]{:S(2)}, u32[]{:S(2)}) collective-permute-start(bf16[1,256,256]{2,1,0:T(8,128)(2,1)S(1)} %get-tuple-element.107), channel_id=1, source_target_pairs={{0,1},{1,2},{2,3},{3,4},{4,5},{5,6},{6,7},{7,8},{8,9},{9,10},{10,1... | collective-permute-start | bytes 393224 | tf_op jit(solution)/shard_map/ppermute | solution.py:12
  18.6 1.9 collective-permute-start.1
  20.6 8.2 %collective-permute-done.1 = bf16[1,256,256]{2,1,0:T(8,128)(2,1)S(1)} collective-permute-done((bf16[1,256,256]{2,1,0:T(8,128)(2,1)S(1)}, bf16[1,256,256]{2,1,0:T(8,128)(2,1)S(1)}, u32[]{:S(2)}, u32[]{:S(2)}) %collective-permute-start.1) | collective-permute-done | bytes 131104 | tf_op jit(solution)/shard_map/ppermute | solution.py:15
  28.8 0.1 fusion.6
  29.4 61.0 %all-gather.3.cloned.1.call-done = bf16[2304,256]{1,0:T(8,128)(2,1)} async-done(((bf16[144,256]{1,0:T(8,128)(2,1)}), bf16[2304,256]{1,0:T(8,128)(2,1)}) %all-gather.3.cloned.1.call-update) | async-done | bytes 1179664 | tf_op jit(solution)/shard_map/all_gather | solution.py:37
  90.4 2.1 fusion.14
  92.5 17.7 %collective-permute-start.2 = (bf16[1,256,256]{2,1,0:T(8,128)(2,1)S(1)}, bf16[1,256,256]{2,1,0:T(8,128)(2,1)S(1)}, u32[]{:S(2)}, u32[]{:S(2)}) collective-permute-start(bf16[1,256,256]{2,1,0:T(8,128)(2,1)S(1)} %get-tuple-element.105), channel_id=1, source_target_pairs={{0,1},{1,2},{2,3},{3,4},{4,5},{5,6},{6,7},{7,8},{8,9},{9,10},{10,1... | collective-permute-start | bytes 393224 | tf_op jit(solution)/shard_map/ppermute | solution.py:12
  110.2 1.9 collective-permute-start.3
  112.9 0.7 fusion.25
  113.7 6.8 %collective-permute-done.3 = bf16[1,256,256]{2,1,0:T(8,128)(2,1)S(1)} collective-permute-done((bf16[1,256,256]{2,1,0:T(8,128)(2,1)S(1)}, bf16[1,256,256]{2,1,0:T(8,128)(2,1)S(1)}, u32[]{:S(2)}, u32[]{:S(2)}) %collective-permute-start.3) | collective-permute-done | bytes 131104 | tf_op jit(solution)/shard_map/ppermute | solution.py:15
  120.5 0.1 select_maximum_fusion
  120.6 0.2 fusion.27
  120.8 0.8 constant_dynamic-update-slice_fusion.9
  121.7 0.8 constant_dynamic-update-slice_fusion.8
  122.4 0.7 constant_dynamic-update-slice_fusion.7
  123.2 0.7 constant_dynamic-update-slice_fusion.6
  123.9 0.8 constant_dynamic-update-slice_fusion.5
  124.7 0.7 constant_dynamic-update-slice_fusion.4
  125.4 0.7 constant_dynamic-update-slice_fusion.3
  126.1 0.8 constant_dynamic-update-slice_fusion.2
  126.9 0.8 constant_dynamic-update-slice_fusion.1
  127.7 48.5 %all-gather.5.cloned.1.call-done = bf16[2304,256]{1,0:T(8,128)(2,1)} async-done(((bf16[144,256]{1,0:T(8,128)(2,1)}), bf16[2304,256]{1,0:T(8,128)(2,1)}) %all-gather.5.cloned.1.call-update) | async-done | bytes 1179664 | tf_op jit(solution)/shard_map/all_gather | solution.py:37
  176.2 2.8 fusion
  179.0 0.2 convolution_convert_fusion
  179.2 36.0 %all_gather.11 = bf16[16,8,2,256]{3,1,2,0:T(8,128)(2,1)S(1)} all-gather(bf16[1,8,2,256]{3,1,2,0:T(8,128)(2,1)S(1)} %bitcast.56), channel_id=1, replica_groups=mesh['member'=16,'lat'=32] {'member'}, dimensions={0}, use_global_device_ids=true | all-gather | bytes 139264 | tf_op jit(solution)/shard_map/all_gather | solution.py:63
  215.3 3.4 %while.14 = (s32[]{:T(128)}, f32[8,2,256]{2,1,0:T(2,128)S(1)}, f32[16,8,2,256]{3,2,1,0:T(2,128)S(1)}, s32[]{:T(128)}, s32[]{:T(128)}) while((s32[]{:T(128)}, f32[8,2,256]{2,1,0:T(2,128)S(1)}, f32[16,8,2,256]{3,2,1,0:T(2,128)S(1)}, s32[]{:T(128)}, s32[]{:T(128)}) %tuple.48), condition=%wide.region_3.4_spmd.clone, body=%wide.region_1.3_spmd.clone.sunk | while | flops 200707 | bytes 376907 | solution.py:70
  215.3 0.2 abs_reduce_fusion.3
  215.6 0.2 abs_reduce_fusion.3
  215.8 0.2 abs_reduce_fusion.3
  216.0 0.2 abs_reduce_fusion.3
  216.2 0.2 abs_reduce_fusion.3
  216.4 0.2 abs_reduce_fusion.3
  216.6 0.2 abs_reduce_fusion.3
  216.8 0.2 abs_reduce_fusion.3
  217.1 0.2 abs_reduce_fusion.3
  217.3 0.2 abs_reduce_fusion.3
  217.5 0.2 abs_reduce_fusion.3
  217.7 0.2 abs_reduce_fusion.3
  217.9 0.2 abs_reduce_fusion.3
  218.1 0.2 abs_reduce_fusion.3
  218.4 0.2 abs_reduce_fusion.3
  218.6 0.2 abs_reduce_fusion.3
  218.8 0.7 multiply_reduce_fusion
  219.5 0.6 copy.16
  220.1 102.5 %all-reduce.2 = (f32[]{:T(128)}, f32[]{:T(128)}) all-reduce(f32[]{:T(128)} %get-tuple-element.95, f32[]{:T(128)} %fusion.25), channel_id=1, replica_groups=mesh['member'=16,'lat'=32] {'lat'}, use_global_device_ids=true, to_apply=%region_5.6 | all-reduce | flops 2 | bytes 16 | tf_op jit(solution)/shard_map/psum | solution.py:74
  (63 shorter events, 1.3 us)
Async XLA Ops:
  7.2 1.5 copy-start
  7.2 21.9 %copy-start.1 = (bf16[1,2,256,256]{3,2,1,0:T(8,128)(2,1)S(1)}, bf16[1,2,256,256]{3,2,1,0:T(8,128)(2,1)}, u32[]{:S(2)}) copy-start(bf16[1,2,256,256]{3,2,1,0:T(8,128)(2,1)} %param.10) | copy-start | bytes 786436
  7.2 83.2 %all-gather.3.cloned.1.call-start = ((), (), s32[]{:S(2)}) async-start(), calls=%async_computation | async-start | bytes 1253376 | tf_op jit(solution)/shard_map/all_gather | solution.py:37
  7.9 168.3 %all-gather.5.cloned.1.call-start = ((), (), s32[]{:S(2)}) async-start(), calls=%async_computation.1 | async-start | bytes 1253376 | tf_op jit(solution)/shard_map/all_gather | solution.py:37
  9.8 10.8 %collective-permute-start = (bf16[1,256,256]{2,1,0:T(8,128)(2,1)S(1)}, bf16[1,256,256]{2,1,0:T(8,128)(2,1)S(1)}, u32[]{:S(2)}, u32[]{:S(2)}) collective-permute-start(bf16[1,256,256]{2,1,0:T(8,128)(2,1)S(1)} %get-tuple-element.107), channel_id=1, source_target_pairs={{0,1},{1,2},{2,3},{3,4},{4,5},{5,6},{6,7},{7,8},{8,9},{9,10},{10,1... | collective-permute-start | bytes 393224 | tf_op jit(solution)/shard_map/ppermute | solution.py:12
  18.6 10.2 %collective-permute-start.1 = (bf16[1,256,256]{2,1,0:T(8,128)(2,1)S(1)}, bf16[1,256,256]{2,1,0:T(8,128)(2,1)S(1)}, u32[]{:S(2)}, u32[]{:S(2)}) collective-permute-start(bf16[1,256,256]{2,1,0:T(8,128)(2,1)S(1)} %get-tuple-element.108), channel_id=1, source_target_pairs={{1,0},{2,1},{3,2},{4,3},{5,4},{6,5},{7,6},{8,7},{9,8},{10,9},{11,1... | collective-permute-start | bytes 393224 | tf_op jit(solution)/shard_map/ppermute | solution.py:15
  90.4 21.8 %copy-start.2 = (f32[8,2,256]{2,1,0:T(2,128)S(1)}, f32[8,2,256]{2,1,0:T(2,128)}, u32[]{:S(2)}) copy-start(f32[8,2,256]{2,1,0:T(2,128)} %param.16) | copy-start | bytes 49156
  92.5 21.1 %collective-permute-start.2 = (bf16[1,256,256]{2,1,0:T(8,128)(2,1)S(1)}, bf16[1,256,256]{2,1,0:T(8,128)(2,1)S(1)}, u32[]{:S(2)}, u32[]{:S(2)}) collective-permute-start(bf16[1,256,256]{2,1,0:T(8,128)(2,1)S(1)} %get-tuple-element.105), channel_id=1, source_target_pairs={{0,1},{1,2},{2,3},{3,4},{4,5},{5,6},{6,7},{7,8},{8,9},{9,10},{10,1... | collective-permute-start | bytes 393224 | tf_op jit(solution)/shard_map/ppermute | solution.py:12
  110.2 10.3 %collective-permute-start.3 = (bf16[1,256,256]{2,1,0:T(8,128)(2,1)S(1)}, bf16[1,256,256]{2,1,0:T(8,128)(2,1)S(1)}, u32[]{:S(2)}, u32[]{:S(2)}) collective-permute-start(bf16[1,256,256]{2,1,0:T(8,128)(2,1)S(1)} %get-tuple-element.106), channel_id=1, source_target_pairs={{1,0},{2,1},{3,2},{4,3},{5,4},{6,5},{7,6},{8,7},{9,8},{10,9},{11,1... | collective-permute-start | bytes 393224 | tf_op jit(solution)/shard_map/ppermute | solution.py:15
  127.7 51.3 %copy-start.3 = (bf16[256,8]{0,1:T(8,128)(2,1)S(1)}, bf16[256,8]{0,1:T(8,128)(2,1)}, u32[]{:S(2)}) copy-start(bf16[256,8]{0,1:T(8,128)(2,1)} %param.15) | copy-start | bytes 12292
Sparse Core Ops, SparseCore 0:
  10.1 80.2 all-gather.2
  92.5 83.7 all-gather.4
where the time goes:
time: 332 us
  blocking collectives  139 us (42%)
  waiting for transfers between devices  125 us (38%)
  starting transfers between devices  30.4 us (9%)
  between operations  18.1 us (5%)
  local copies, waits for them, and re-layouts  8.13 us (2%)
  other arithmetic  5.8 us (2%)
  matrix products  5.15 us (2%)
    all_gather x2, waiting for transfers between devices, folded_conv(): lax.all_gather(weight_rows, 'member', axis=0, tiled=True)  110 us
    psum x1, blocking collectives, body(): lax.psum((jnp.sum(score * area[None, :, None]), jnp.sum(area)), 'lat')  102 us
    all_gather x1, blocking collectives, body(): lax.all_gather(pred[None], 'member', axis=0, tiled=True).astype(jnp.float32)  36 us
    ppermute x2, starting transfers between devices, with_halo(): lax.ppermute(lax.slice_in_dim(block, block.shape[dim] - width, None, axis...  26.5 us
    ppermute x2, waiting for transfers between devices, with_halo(): lax.ppermute(lax.slice_in_dim(block, 0, width, axis=dim), axis, backward)  15.1 us
    unnamed x24, local copies, waits for them, and re-layouts  6.93 us
  transfers between devices with their start and end apart: 6, of which 4 were waited for; matrix products, arithmetic and copies ran while one was open for 4% of the time, Pallas kernels for 0%

commit v1 on v0

--- a/solution.py
+++ b/solution.py
@@ -34,7 +34,16 @@
 
 
 def folded_conv(patches, weight_rows):
-    return product(patches, lax.all_gather(weight_rows, "member", axis=0, tiled=True))
+    plane_load = lambda z: jnp.concatenate(
+        lax.all_to_all(
+            jnp.stack(lax.axis_size("member") * [z]),
+            axis_name="member",
+            split_axis=0,
+            concat_axis=0,
+        ),
+        axis=0,
+    )
+    return product(patches, plane_load(weight_rows))
 
 
 def body(states, member_id, member_gain, first_conv, second_conv, head, target, lat_start):

time: 332 us -> 229 us (0.69)
  waiting for transfers between devices: 125 us -> 35.5 us
  between operations: 18.1 us -> 4.5 us
  local copies, waits for them, and re-layouts: 8.13 us -> 15.7 us
  blocking collectives: 139 us -> 132 us
    all_gather x2 -> x0, waiting for transfers between devices: 110 us -> none  [folded_conv(): lax.all_gather(weight_rows, 'member', axis=0, tiled=True)]
    ppermute x2, waiting for transfers between devices: 0.01 us -> 22.3 us  [with_halo(): lax.ppermute(lax.slice_in_dim(block, block.shape[dim] - width, None, axis...]
    ppermute x2, starting transfers between devices: 26.5 us -> 9.37 us  [with_halo(): lax.ppermute(lax.slice_in_dim(block, block.shape[dim] - width, None, axis...]
    all_to_all x0 -> x2, starting transfers between devices: none -> 15 us  [folded_conv(): lax.all_to_all(jnp.stack(lax.axis_size('member') * [z]), axis_name='membe...]
    ppermute x2, waiting for transfers between devices: 15.1 us -> 8.24 us  [with_halo(): lax.ppermute(lax.slice_in_dim(block, 0, width, axis=dim), axis, backward)]
    all_to_all x0 -> x2, waiting for transfers between devices: none -> 4.91 us  [folded_conv(): lax.all_to_all(jnp.stack(lax.axis_size('member') * [z]), axis_name='membe...]
    psum x1, blocking collectives: 102 us -> 98.2 us  [body(): lax.psum((jnp.sum(score * area[None, :, None]), jnp.sum(area)), 'lat')]
    unnamed x24 -> x26, local copies, waits for them, and re-layouts: 6.93 us -> 10.7 us
  transfers between devices with their start and end apart: 6 -> 6, of which waited for: 4 -> 5; matrix products, arithmetic and copies ran while one was open for 4% -> 8% of each run, Pallas kernels for 0% -> 0%
where the time goes in v1:
time: 229 us; the launch traced here: 228 us
  blocking collectives  132 us (58%)
  waiting for transfers between devices  35.5 us (16%)
  starting transfers between devices  28.2 us (12%)
  local copies, waits for them, and re-layouts  15.7 us (7%)
  other arithmetic  6.91 us (3%)
  matrix products  5.22 us (2%)
  between operations  4.5 us (2%)
    psum x1, blocking collectives, body(): lax.psum((jnp.sum(score * area[None, :, None]), jnp.sum(area)), 'lat')  98.2 us
    all_gather x1, blocking collectives, body(): lax.all_gather(pred[None], 'member', axis=0, tiled=True).astype(jnp.float32)  33.7 us
    ppermute x2, waiting for transfers between devices, with_halo(): lax.ppermute(lax.slice_in_dim(block, block.shape[dim] - width, None, axis...  22.3 us
    all_to_all x2, starting transfers between devices, folded_conv(): lax.all_to_all(jnp.stack(lax.axis_size('member') * [z]), axis_name='membe...  15 us
    unnamed x26, local copies, waits for them, and re-layouts  10.7 us
    ppermute x2, starting transfers between devices, with_halo(): lax.ppermute(lax.slice_in_dim(block, block.shape[dim] - width, None, axis...  9.37 us
    ppermute x2, waiting for transfers between devices, with_halo(): lax.ppermute(lax.slice_in_dim(block, 0, width, axis=dim), axis, backward)  8.24 us
    dot_general x3, matrix products, product(): jnp.dot(left.astype(jnp.float32), right.astype(jnp.float32), precision=la...  5.1 us
  transfers between devices with their start and end apart: 6, of which 5 were waited for; matrix products, arithmetic and copies ran while one was open for 8% of the time, Pallas kernels for 0%

profile of v1, /device:TPU:1, one launch (start us, length us, event | category | flops | bytes accessed | tf_op | source)
XLA Modules:
  0.0 228.5 jit_solution(6731009335334009826)
XLA Ops:
  0.7 2.0 stack.4
  2.7 8.0 %all-to-all-start = ((bf16[16,144,256]{2,1,0:T(8,128)(2,1)}), bf16[16,144,256]{2,1,0:T(8,128)(2,1)S(1)}, u32[]{:S(2)}, u32[]{:S(2)}) async-start(bf16[16,144,256]{2,1,0:T(8,128)(2,1)} %stack.4), calls=%async_computation | async-start | bytes 2359296 | tf_op jit(solution)/shard_map/all_to_all | solution.py:38
  11.5 5.6 %collective-permute-start = (bf16[1,256,256]{2,1,0:T(8,128)(2,1)S(1)}, bf16[1,256,256]{2,1,0:T(8,128)(2,1)S(1)}, u32[]{:S(2)}, u32[]{:S(2)}) collective-permute-start(bf16[1,256,256]{2,1,0:T(8,128)(2,1)S(1)} %get-tuple-element.107), channel_id=1, source_target_pairs={{0,1},{1,2},{2,3},{3,4},{4,5},{5,6},{6,7},{7,8},{8,9},{9,10},{10,1... | collective-permute-start | bytes 393224 | tf_op jit(solution)/shard_map/ppermute | solution.py:12
  17.1 1.9 collective-permute-start.1
  19.1 11.9 %collective-permute-done = bf16[1,256,256]{2,1,0:T(8,128)(2,1)S(1)} collective-permute-done((bf16[1,256,256]{2,1,0:T(8,128)(2,1)S(1)}, bf16[1,256,256]{2,1,0:T(8,128)(2,1)S(1)}, u32[]{:S(2)}, u32[]{:S(2)}) %collective-permute-start) | collective-permute-done | bytes 131104 | tf_op jit(solution)/shard_map/ppermute | solution.py:12
  30.9 6.9 %collective-permute-done.1 = bf16[1,256,256]{2,1,0:T(8,128)(2,1)S(1)} collective-permute-done((bf16[1,256,256]{2,1,0:T(8,128)(2,1)S(1)}, bf16[1,256,256]{2,1,0:T(8,128)(2,1)S(1)}, u32[]{:S(2)}, u32[]{:S(2)}) %collective-permute-start.1) | collective-permute-done | bytes 131104 | tf_op jit(solution)/shard_map/ppermute | solution.py:15
  37.9 0.7 slice_dynamic-update-slice_fusion.5
  38.7 0.7 fusion.18
  39.4 0.8 slice_dynamic-update-slice_fusion.4
  40.2 0.8 slice_dynamic-update-slice_fusion.3
  41.0 0.8 constant_dynamic-update-slice_fusion
  41.8 0.8 slice_dynamic-update-slice_fusion.2
  42.6 0.7 slice_dynamic-update-slice_fusion.1
  43.4 0.7 fusion.17
  44.1 0.8 slice_dynamic-update-slice_fusion
  44.9 1.1 stack.5
  46.0 7.0 %all-to-all-start.1 = ((bf16[16,144,256]{2,1,0:T(8,128)(2,1)}), bf16[16,144,256]{2,1,0:T(8,128)(2,1)S(1)}, u32[]{:S(2)}, u32[]{:S(2)}) async-start(bf16[16,144,256]{2,1,0:T(8,128)(2,1)} %stack.5), calls=%async_computation.1 | async-start | bytes 2359296 | tf_op jit(solution)/shard_map/all_to_all | solution.py:38
  53.1 2.5 %fusion.14 = bf16[512,256]{1,0:T(8,128)(2,1)S(1)} fusion(bf16[512,2304]{1,0:T(8,128)(2,1)} %bitcast.5, bf16[2304,256]{1,0:T(8,128)(2,1)S(1)} %bitcast.51), kind=kOutput, calls=%fused_computation.24 | convolution fusion | flops 605159424 | bytes 3801088 | tf_op jit(solution)/shard_map/dot_general | solution.py:21
  55.6 3.8 %collective-permute-start.2 = (bf16[1,256,256]{2,1,0:T(8,128)(2,1)S(1)}, bf16[1,256,256]{2,1,0:T(8,128)(2,1)S(1)}, u32[]{:S(2)}, u32[]{:S(2)}) collective-permute-start(bf16[1,256,256]{2,1,0:T(8,128)(2,1)S(1)} %get-tuple-element.105), channel_id=1, source_target_pairs={{0,1},{1,2},{2,3},{3,4},{4,5},{5,6},{6,7},{7,8},{8,9},{9,10},{10,1... | collective-permute-start | bytes 393224 | tf_op jit(solution)/shard_map/ppermute | solution.py:12
  59.4 1.9 collective-permute-start.3
  62.1 0.7 fusion.25
  62.8 10.5 %collective-permute-done.2 = bf16[1,256,256]{2,1,0:T(8,128)(2,1)S(1)} collective-permute-done((bf16[1,256,256]{2,1,0:T(8,128)(2,1)S(1)}, bf16[1,256,256]{2,1,0:T(8,128)(2,1)S(1)}, u32[]{:S(2)}, u32[]{:S(2)}) %collective-permute-start.2) | collective-permute-done | bytes 131104 | tf_op jit(solution)/shard_map/ppermute | solution.py:12
  73.2 1.4 collective-permute-done.3
  74.7 0.2 fusion.27
  74.9 0.7 constant_dynamic-update-slice_fusion.9
  75.7 0.7 constant_dynamic-update-slice_fusion.8
  76.5 0.8 constant_dynamic-update-slice_fusion.7
  77.2 0.8 constant_dynamic-update-slice_fusion.6
  78.0 0.8 constant_dynamic-update-slice_fusion.5
  78.8 0.8 constant_dynamic-update-slice_fusion.4
  79.6 0.7 constant_dynamic-update-slice_fusion.3
  80.3 0.7 constant_dynamic-update-slice_fusion.2
  81.0 0.8 constant_dynamic-update-slice_fusion.1
  81.8 4.9 %all-to-all-done.1 = bf16[16,144,256]{2,1,0:T(8,128)(2,1)S(1)} async-done(((bf16[16,144,256]{2,1,0:T(8,128)(2,1)}), bf16[16,144,256]{2,1,0:T(8,128)(2,1)S(1)}, u32[]{:S(2)}, u32[]{:S(2)}) %all-to-all-start.1) | async-done | bytes 1179680 | tf_op jit(solution)/shard_map/all_to_all | solution.py:38
  86.7 2.4 %fusion = bf16[512,256]{1,0:T(8,128)(2,1)S(1)} fusion(bf16[512,2304]{1,0:T(8,128)(2,1)} %constant_dynamic-update-slice_fusion.1, bf16[2304,256]{1,0:T(8,128)(2,1)S(1)} %bitcast.50, bf16[512,256]{1,0:T(8,128)(2,1)S(1)} %fusion.16), kind=kOutput, calls=%fused_computation.6 | convolution fusion | flops 604372992 | bytes 4063232 | tf_op jit(solution)/shard_map/dot_general | solution.py:21
  89.2 0.2 convolution_convert_fusion
  89.3 33.7 %all_gather.3 = bf16[16,8,2,256]{3,1,2,0:T(8,128)(2,1)S(1)} all-gather(bf16[1,8,2,256]{3,1,2,0:T(8,128)(2,1)S(1)} %bitcast.60), channel_id=1, replica_groups=mesh['member'=16,'lat'=32] {'member'}, dimensions={0}, use_global_device_ids=true | all-gather | bytes 139264 | tf_op jit(solution)/shard_map/all_gather | solution.py:72
  123.1 3.4 %while.14 = (s32[]{:T(128)}, f32[8,2,256]{2,1,0:T(2,128)S(1)}, f32[16,8,2,256]{3,2,1,0:T(2,128)S(1)}, s32[]{:T(128)}, s32[]{:T(128)}) while((s32[]{:T(128)}, f32[8,2,256]{2,1,0:T(2,128)S(1)}, f32[16,8,2,256]{3,2,1,0:T(2,128)S(1)}, s32[]{:T(128)}, s32[]{:T(128)}) %tuple.48), condition=%wide.region_3.4_spmd.clone, body=%wide.region_1.3_spmd.clone.sunk | while | flops 200707 | bytes 376907 | solution.py:79
  123.3 0.2 abs_reduce_fusion.3
  123.5 0.2 abs_reduce_fusion.3
  123.8 0.2 abs_reduce_fusion.3
  124.0 0.2 abs_reduce_fusion.3
  124.8 0.2 abs_reduce_fusion.3
  125.0 0.2 abs_reduce_fusion.3
  125.3 0.2 abs_reduce_fusion.3
  126.6 0.7 multiply_reduce_fusion
  127.2 0.6 copy.16
  127.9 98.2 %all-reduce.2 = (f32[]{:T(128)}, f32[]{:T(128)}) all-reduce(f32[]{:T(128)} %get-tuple-element.95, f32[]{:T(128)} %fusion.25), channel_id=1, replica_groups=mesh['member'=16,'lat'=32] {'lat'}, use_global_device_ids=true, to_apply=%region_5.6 | all-reduce | flops 2 | bytes 16 | tf_op jit(solution)/shard_map/psum | solution.py:83
  (65 shorter events, 2.7 us)
Async XLA Ops:
  0.6 10.7 %copy-start = (f32[16,256]{1,0:T(8,128)S(1)}, f32[16,256]{1,0:T(8,128)}, u32[]{:S(2)}) copy-start(f32[16,256]{1,0:T(8,128)} %param.12) | copy-start | bytes 49156
  0.6 10.8 %copy-start.1 = (bf16[1,2,256,256]{3,2,1,0:T(8,128)(2,1)S(1)}, bf16[1,2,256,256]{3,2,1,0:T(8,128)(2,1)}, u32[]{:S(2)}) copy-start(bf16[1,2,256,256]{3,2,1,0:T(8,128)(2,1)} %param.10) | copy-start | bytes 786436
  2.7 42.2 %all-to-all-start = ((bf16[16,144,256]{2,1,0:T(8,128)(2,1)}), bf16[16,144,256]{2,1,0:T(8,128)(2,1)S(1)}, u32[]{:S(2)}, u32[]{:S(2)}) async-start(bf16[16,144,256]{2,1,0:T(8,128)(2,1)} %stack.4), calls=%async_computation | async-start | bytes 2359296 | tf_op jit(solution)/shard_map/all_to_all | solution.py:38
  11.5 19.4 %collective-permute-start = (bf16[1,256,256]{2,1,0:T(8,128)(2,1)S(1)}, bf16[1,256,256]{2,1,0:T(8,128)(2,1)S(1)}, u32[]{:S(2)}, u32[]{:S(2)}) collective-permute-start(bf16[1,256,256]{2,1,0:T(8,128)(2,1)S(1)} %get-tuple-element.107), channel_id=1, source_target_pairs={{0,1},{1,2},{2,3},{3,4},{4,5},{5,6},{6,7},{7,8},{8,9},{9,10},{10,1... | collective-permute-start | bytes 393224 | tf_op jit(solution)/shard_map/ppermute | solution.py:12
  17.1 20.7 %collective-permute-start.1 = (bf16[1,256,256]{2,1,0:T(8,128)(2,1)S(1)}, bf16[1,256,256]{2,1,0:T(8,128)(2,1)S(1)}, u32[]{:S(2)}, u32[]{:S(2)}) collective-permute-start(bf16[1,256,256]{2,1,0:T(8,128)(2,1)S(1)} %get-tuple-element.108), channel_id=1, source_target_pairs={{1,0},{2,1},{3,2},{4,3},{5,4},{6,5},{7,6},{8,7},{9,8},{10,9},{11,1... | collective-permute-start | bytes 393224 | tf_op jit(solution)/shard_map/ppermute | solution.py:15
  38.7 6.2 %copy-start.2 = (bf16[144,256]{1,0:T(8,128)(2,1)S(1)}, bf16[144,256]{1,0:T(8,128)(2,1)}, u32[]{:S(2)}) copy-start(bf16[144,256]{1,0:T(8,128)(2,1)} %param.14) | copy-start | bytes 221188
  46.0 40.7 %all-to-all-start.1 = ((bf16[16,144,256]{2,1,0:T(8,128)(2,1)}), bf16[16,144,256]{2,1,0:T(8,128)(2,1)S(1)}, u32[]{:S(2)}, u32[]{:S(2)}) async-start(bf16[16,144,256]{2,1,0:T(8,128)(2,1)} %stack.5), calls=%async_computation.1 | async-start | bytes 2359296 | tf_op jit(solution)/shard_map/all_to_all | solution.py:38
  53.1 8.3 %copy-start.3 = (f32[8,2,256]{2,1,0:T(2,128)S(1)}, f32[8,2,256]{2,1,0:T(2,128)}, u32[]{:S(2)}) copy-start(f32[8,2,256]{2,1,0:T(2,128)} %param.16) | copy-start | bytes 49156
  55.6 17.6 %collective-permute-start.2 = (bf16[1,256,256]{2,1,0:T(8,128)(2,1)S(1)}, bf16[1,256,256]{2,1,0:T(8,128)(2,1)S(1)}, u32[]{:S(2)}, u32[]{:S(2)}) collective-permute-start(bf16[1,256,256]{2,1,0:T(8,128)(2,1)S(1)} %get-tuple-element.105), channel_id=1, source_target_pairs={{0,1},{1,2},{2,3},{3,4},{4,5},{5,6},{6,7},{7,8},{8,9},{9,10},{10,1... | collective-permute-start | bytes 393224 | tf_op jit(solution)/shard_map/ppermute | solution.py:12
  59.4 15.2 %collective-permute-start.3 = (bf16[1,256,256]{2,1,0:T(8,128)(2,1)S(1)}, bf16[1,256,256]{2,1,0:T(8,128)(2,1)S(1)}, u32[]{:S(2)}, u32[]{:S(2)}) collective-permute-start(bf16[1,256,256]{2,1,0:T(8,128)(2,1)S(1)} %get-tuple-element.106), channel_id=1, source_target_pairs={{1,0},{2,1},{3,2},{4,3},{5,4},{6,5},{7,6},{8,7},{9,8},{10,9},{11,1... | collective-permute-start | bytes 393224 | tf_op jit(solution)/shard_map/ppermute | solution.py:15
  81.8 7.4 %copy-start.4 = (bf16[256,8]{0,1:T(8,128)(2,1)S(1)}, bf16[256,8]{0,1:T(8,128)(2,1)}, u32[]{:S(2)}) copy-start(bf16[256,8]{0,1:T(8,128)(2,1)} %param.15) | copy-start | bytes 12292
